TPU v7x, 32 devices: a whole 2x2x4 slice. The times are simulated.
32 devices in a mesh: dp: 2 (over x), expert: 16 (over z, y, core).
Axes of the slice: x: 2, y: 2, z: 4, core: 2. Of those that a mesh axis runs over, the one named last changes fastest.
Arguments:
- tokens: bfloat16 [512, 2048], P('expert', 'dp'), may hold values from -6 to 6
- cotangent: bfloat16 [512, 2048], P('expert', 'dp'), may hold values from -6 to 6
- routes: int32 [512, 8], P('expert'), may hold values from 0 to 15, all different within a row; in each aligned block of 32 rows (0 to 31, 32 to 63, ...) at most 20 rows name the same one
- probs: float32 [512, 8], P('expert'), may hold values from 0.03 to 0.6
- matching: int32 [16], replicated, may hold values from 0 to 15, as said below
- gate_weight: bfloat16 [16, 2048, 1024], P('expert', None, 'dp'), may hold values from -0.125 to 0.125
- up_weight: bfloat16 [16, 2048, 1024], P('expert', None, 'dp'), may hold values from -0.125 to 0.125
- down_weight: bfloat16 [16, 2048, 1024], P('expert', None, 'dp'), may hold values from -0.1875 to 0.1875
Outputs:
- input_grad: bfloat16 [512, 2048], P('expert', 'dp')
- gate_weight_grad: float32 [16, 2048, 1024], P('expert', None, 'dp')
- up_weight_grad: float32 [16, 2048, 1024], P('expert', None, 'dp')
- down_weight_grad: float32 [16, 2048, 1024], P('expert', None, 'dp')
Inputs may be any that keep to these rules, and one draw needn't show every extreme that they name: matching pairs the experts: matching[matching[i]] == i and matching[i] != i. `routes`: each token names 8 different experts; within each aligned block of 32 tokens no expert is named by more than 20 tokens.
All inputs are finite; a program needn't handle non-finite values.
Results may differ from a plain program's by a relative error of at most 0.015.
Values may be sent and summed in bfloat16 or wider, within the bound.
A program may use at most 64 MiB of HBM per device.

v0:
```python
import jax
import jax.numpy as jnp
from jax import lax
from jax.sharding import PartitionSpec as P

contract_rows = (((0,), (0,)), ((), ()))
contract_cols = (((1,), (1,)), ((), ()))


def pair_rows(cotangent, routes, probs, expert):
    weight = jnp.sum(jnp.where(routes == expert, probs, 0.0), axis=1)
    return (cotangent.astype(jnp.float32) * weight[:, None]).astype(jnp.bfloat16)


def local(tokens, cotangent, routes, probs, matching, gate_weight, up_weight, down_weight):
    experts = matching.shape[0]
    tok_rows = routes.shape[0]
    hidden_width = gate_weight.shape[2]
    me = lax.axis_index("expert")
    w_gate, w_up, w_down = (gate_weight[0], up_weight[0], down_weight[0])
    routes_all = lax.all_gather(routes, "expert", axis=0, tiled=True)
    probs_all = lax.all_gather(probs, "expert", axis=0, tiled=True)
    both = jnp.stack([tokens, cotangent], axis=0)
    both = lax.all_gather(both, "dp", axis=2, tiled=True)
    both = lax.all_gather(both, "expert", axis=1, tiled=True)
    rows, cot = (both[0], both[1])
    grads = pair_rows(cot, routes_all, probs_all, me)
    gate = jnp.dot(rows, w_gate, preferred_element_type=jnp.float32)
    upper = jnp.dot(rows, w_up, preferred_element_type=jnp.float32)
    sig = jax.nn.sigmoid(gate)
    hidden = (gate * sig * upper).astype(jnp.bfloat16)
    hidden_back = jnp.dot(grads, w_down, preferred_element_type=jnp.float32)
    up_back = (hidden_back * gate * sig).astype(jnp.bfloat16)
    gate_back = (hidden_back * upper * sig * (1.0 + gate * (1.0 - sig))).astype(jnp.bfloat16)
    packed = jnp.concatenate([gate_back, up_back, hidden], axis=1)
    packed = packed.reshape(experts, tok_rows, 3 * hidden_width)
    spread = lax.all_to_all(packed, "expert", split_axis=0, concat_axis=0, tiled=True)
    ordered = jnp.take(spread, matching, axis=0)
    landed = lax.all_to_all(ordered, "expert", split_axis=0, concat_axis=0, tiled=True)
    landed = landed.reshape(experts * tok_rows, 3 * hidden_width)
    part = lax.dot_general(gate_back, w_gate, contract_cols, preferred_element_type=jnp.float32)
    part = part + lax.dot_general(up_back, w_up, contract_cols, preferred_element_type=jnp.float32)
    part = part.astype(jnp.bfloat16)
    summed = lax.psum_scatter(part, "dp", scatter_dimension=1, tiled=True)
    summed = summed.reshape(experts, tok_rows, summed.shape[1])
    back = lax.all_to_all(summed, "expert", split_axis=0, concat_axis=0, tiled=True)
    input_grad = jnp.sum(back.astype(jnp.float32), axis=0).astype(jnp.bfloat16)
    partner = matching[me]
    p_grads = pair_rows(cot, routes_all, probs_all, partner)
    g_gate = lax.dot_general(
        rows, landed[:, :hidden_width], contract_rows, preferred_element_type=jnp.float32
    )
    g_up = lax.dot_general(
        rows,
        landed[:, hidden_width : 2 * hidden_width],
        contract_rows,
        preferred_element_type=jnp.float32,
    )
    g_down = lax.dot_general(
        p_grads, landed[:, 2 * hidden_width :], contract_rows, preferred_element_type=jnp.float32
    )
    return (input_grad, g_gate[None], g_up[None], g_down[None])


def solution(mesh):
    placed = (
        P("expert", "dp"),
        P("expert", "dp"),
        P("expert", None),
        P("expert", None),
        P(),
        P("expert", None, "dp"),
        P("expert", None, "dp"),
        P("expert", None, "dp"),
    )
    return jax.shard_map(
        local,
        mesh=mesh,
        in_specs=placed,
        out_specs=(
            P("expert", "dp"),
            P("expert", None, "dp"),
            P("expert", None, "dp"),
            P("expert", None, "dp"),
        ),
        check_vma=False,
    )
```

profile of v0, /device:TPU:9, one launch (start us, length us, event | category | flops | bytes accessed | tf_op | source)
XLA Modules:
  0.0 202.9 jit_solution(15081266872429991125)
XLA Ops:
  7.2 0.0 copy-start
  7.2 0.0 all-gather.4.cloned.1.call-start
  7.2 1.0 pad_maximum_fusion.1
  8.3 5.1 %all_gather.12 = bf16[2,32,2048]{2,1,0:T(8,128)(2,1)} all-gather(bf16[2,32,1024]{2,1,0:T(8,128)(2,1)S(1)} %pad_maximum_fusion.1), channel_id=1, replica_groups=mesh['dp'=2,'expert'=16] {'dp'}, dimensions={2}, use_global_device_ids=true | all-gather | bytes 393216 | tf_op jit(solution)/shard_map/all_gather | solution.py:24
  13.4 0.0 all-gather.4.cloned.1.call-update
  13.4 1.2 dynamic_slice.3
  14.7 20.8 %all-gather = s32[16,32,8]{1,2,0:T(8,128)S(1)} all-gather(s32[1,32,8]{1,2,0:T(8,128)} %bitcast.53), channel_id=1, replica_groups=mesh['dp'=2,'expert'=16] {'expert'}, dimensions={0}, use_global_device_ids=true | all-gather | bytes 17408 | tf_op jit(solution)/shard_map/all_gather | solution.py:21
  35.5 18.5 %all-gather.1 = f32[16,32,8]{1,2,0:T(8,128)S(1)} all-gather(f32[1,32,8]{1,2,0:T(8,128)} %bitcast.54), channel_id=1, replica_groups=mesh['dp'=2,'expert'=16] {'expert'}, dimensions={0}, use_global_device_ids=true | all-gather | bytes 17408 | tf_op jit(solution)/shard_map/all_gather | solution.py:22
  54.0 0.7 select_reduce_fusion
  54.7 0.1 reshape.57
  54.8 11.9 %all-gather.4.cloned.1.call-done = bf16[2,512,2048]{2,1,0:T(8,128)(2,1)} async-done(((bf16[2,32,2048]{2,1,0:T(8,128)(2,1)}), bf16[2,512,2048]{2,1,0:T(8,128)(2,1)}) %all-gather.4.cloned.1.call-update) | async-done | bytes 4194320 | tf_op jit(solution)/shard_map/all_gather | solution.py:25
  66.7 0.0 copy-start.1
  66.7 0.0 copy-start.3
  66.7 3.7 %fusion.9 = f32[512,512]{0,1:T(8,128)S(1)} fusion(bf16[1,2048,512]{2,1,0:T(8,128)(2,1)} %param.13, bf16[2,512,2048]{2,1,0:T(8,128)(2,1)} %all-gather.4.cloned.1.call-done), kind=kOutput, calls=%fused_computation.15 | convolution fusion | flops 1073741824 | bytes 5242880 | tf_op jit(solution)/shard_map/dot_general | solution.py:28
  70.3 0.0 copy-done.1
  70.3 0.4 copy-done.3
  70.8 1.4 fusion.5
  72.2 0.0 copy-done
  72.2 1.7 multiply_convert_fusion
  73.9 1.2 pad_maximum_fusion
  75.1 2.6 %copy.13 = bf16[512,1536]{1,0:T(8,128)(2,1)} copy(bf16[512,1536]{0,1:T(8,128)(2,1)} %pad_maximum_fusion) | data formatting | bytes 3145728 | tf_op jit(solution)/shard_map/concatenate | solution.py:35
  77.7 4.5 %all-to-all-start.1 = ((bf16[16,32,1536]{2,1,0:T(8,128)(2,1)}), bf16[16,32,1536]{2,1,0:T(8,128)(2,1)}, u32[]{:S(2)}, u32[]{:S(2)}) async-start(bf16[16,32,1536]{2,1,0:T(8,128)(2,1)} %bitcast.49), calls=%async_computation.2 | async-start | bytes 3145728 | tf_op jit(solution)/shard_map/all_to_all | solution.py:37
  82.2 0.0 reduce-scatter.2.cloned.1.call-start
  82.3 2.9 %fusion.7 = f32[512,2048]{1,0:T(8,128)S(1)} fusion(bf16[512,512]{0,1:T(8,128)(2,1)S(1)} %get-tuple-element.7, bf16[1,2048,512]{2,1,0:T(8,128)(2,1)} %param.13), kind=kOutput, calls=%fused_computation.13 | convolution fusion | flops 1073741824 | bytes 6815744 | tf_op jit(solution)/shard_map/dot_general | solution.py:41
  85.2 2.6 %add_convert_fusion = bf16[512,2048]{1,0:T(8,128)(2,1)} fusion(f32[512,2048]{1,0:T(8,128)S(1)} %fusion.7, bf16[512,512]{0,1:T(8,128)(2,1)S(1)} %get-tuple-element.8, bf16[1,2048,512]{2,1,0:T(8,128)(2,1)S(1)} %copy-done), kind=kOutput, calls=%fused_computation.6 | convolution fusion | flops 1075838976 | bytes 8912896 | tf_op jit(solution)/shard_map/dot_general | solution.py:42
  87.8 0.0 copy-start.4
  87.8 0.0 reduce-scatter.2.cloned.1.call-update
  87.8 0.6 copy-done.4
  88.5 29.4 %all-to-all-done.1 = bf16[16,32,1536]{2,1,0:T(8,128)(2,1)} async-done(((bf16[16,32,1536]{2,1,0:T(8,128)(2,1)}), bf16[16,32,1536]{2,1,0:T(8,128)(2,1)}, u32[]{:S(2)}, u32[]{:S(2)}) %all-to-all-start.1) | async-done | bytes 1572896 | tf_op jit(solution)/shard_map/all_to_all | solution.py:37
  117.9 3.2 %gather_fusion = bf16[16,32,1536]{2,1,0:T(8,128)(2,1)} fusion(bf16[16,32,1536]{2,1,0:T(8,128)(2,1)} %all-to-all-done.1, s32[1024]{0:T(1024)S(1)} %pad_clamp_fusion), kind=kCustom, calls=%fused_computation | custom fusion | bytes 3145792 | tf_op jit(solution)/shard_map/jit(_take)/gather | solution.py:38
  121.1 2.8 %broadcast_select_fusion = bf16[16,32,1536]{2,1,0:T(8,128)(2,1)} fusion(bf16[16,32,1536]{2,1,0:T(8,128)(2,1)} %gather_fusion, pred[16]{0:T(512)(128)(4,1)S(1)} %compare_and_fusion), kind=kLoop, calls=%fused_computation.26 | loop fusion | flops 786432 | bytes 3145744 | tf_op jit(solution)/shard_map/jit(_take)/select_n | solution.py:38
  123.9 5.4 %all-to-all-start.2 = ((bf16[16,32,1536]{2,1,0:T(8,128)(2,1)}), bf16[16,32,1536]{2,1,0:T(8,128)(2,1)}, u32[]{:S(2)}, u32[]{:S(2)}) async-start(bf16[16,32,1536]{2,1,0:T(8,128)(2,1)} %broadcast_select_fusion), calls=%async_computation.3 | async-start | bytes 3145728 | tf_op jit(solution)/shard_map/all_to_all | solution.py:39
  129.3 0.0 reduce-scatter.2.cloned.1.call-done
  129.3 35.6 %all-to-all-done.2 = bf16[16,32,1536]{2,1,0:T(8,128)(2,1)} async-done(((bf16[16,32,1536]{2,1,0:T(8,128)(2,1)}), bf16[16,32,1536]{2,1,0:T(8,128)(2,1)}, u32[]{:S(2)}, u32[]{:S(2)}) %all-to-all-start.2) | async-done | bytes 1572896 | tf_op jit(solution)/shard_map/all_to_all | solution.py:39
  164.9 5.4 %all-to-all-start = ((bf16[16,32,1024]{2,1,0:T(8,128)(2,1)}), bf16[16,32,1024]{2,1,0:T(8,128)(2,1)S(1)}, u32[]{:S(2)}, u32[]{:S(2)}) async-start(bf16[16,32,1024]{2,1,0:T(8,128)(2,1)} %bitcast.50), calls=%async_computation.1 | async-start | bytes 2097152 | tf_op jit(solution)/shard_map/all_to_all | solution.py:46
  170.3 0.1 reshape.58
  170.4 0.0 copy-start.2
  170.4 5.1 %convolution_bitcast_fusion.1 = f32[1,2048,512]{2,1,0:T(8,128)} fusion(bf16[2,512,2048]{2,1,0:T(8,128)(2,1)} %all-gather.4.cloned.1.call-done, bf16[512,1536]{1,0:T(8,128)(2,1)} %bitcast.11), kind=kOutput, calls=%fused_computation.8 | convolution fusion | flops 1073741824 | bytes 6815744 | tf_op jit(solution)/shard_map/dot_general | solution.py:53
  175.6 0.0 copy-done.2
  175.6 4.4 %convolution_bitcast_fusion.2 = f32[1,2048,512]{2,1,0:T(8,128)} fusion(bf16[2,512,2048]{2,1,0:T(8,128)(2,1)S(1)} %copy-done.2, bf16[512,1536]{1,0:T(8,128)(2,1)} %bitcast.11), kind=kOutput, calls=%fused_computation.9 | convolution fusion | flops 1073741824 | bytes 6815744 | tf_op jit(solution)/shard_map/dot_general | solution.py:50
  179.9 4.5 %convolution_bitcast_fusion = f32[1,2048,512]{2,1,0:T(8,128)} fusion(f32[512]{0:T(512)S(1)} %reshape.58, bf16[2,512,2048]{2,1,0:T(8,128)(2,1)S(1)} %copy-done.2, bf16[512,1536]{1,0:T(8,128)(2,1)} %bitcast.11), kind=kOutput, calls=%fused_computation.7 | convolution fusion | flops 1076887552 | bytes 6817792 | tf_op jit(solution)/shard_map/dot_general | solution.py:59
  184.4 10.9 %all-to-all-done = bf16[16,32,1024]{2,1,0:T(8,128)(2,1)S(1)} async-done(((bf16[16,32,1024]{2,1,0:T(8,128)(2,1)}), bf16[16,32,1024]{2,1,0:T(8,128)(2,1)S(1)}, u32[]{:S(2)}, u32[]{:S(2)}) %all-to-all-start) | async-done | bytes 1048608 | tf_op jit(solution)/shard_map/all_to_all | solution.py:46
  195.3 0.8 reduce_sum.31
  (3 shorter events, 0.0 us)
Async XLA Ops:
  7.2 65.0 %copy-start = (bf16[1,2048,512]{2,1,0:T(8,128)(2,1)S(1)}, bf16[1,2048,512]{2,1,0:T(8,128)(2,1)}, u32[]{:S(2)}) copy-start(bf16[1,2048,512]{2,1,0:T(8,128)(2,1)} %param.14) | copy-start | bytes 6291460
  7.2 59.5 %all-gather.4.cloned.1.call-start = ((), (), s32[]{:S(2)}) async-start(), calls=%async_computation.4 | async-start | bytes 4456448 | tf_op jit(solution)/shard_map/all_gather | solution.py:25
  66.7 3.7 %copy-start.1 = (bf16[2,512,2048]{2,1,0:T(8,128)(2,1)S(1)}, bf16[2,512,2048]{2,1,0:T(8,128)(2,1)}, u32[]{:S(2)}) copy-start(bf16[2,512,2048]{2,1,0:T(8,128)(2,1)} %all-gather.4.cloned.1.call-done) | copy-start | bytes 12582916
  66.7 4.1 %copy-start.3 = (bf16[1,2048,512]{2,1,0:T(8,128)(2,1)S(1)}, bf16[1,2048,512]{2,1,0:T(8,128)(2,1)}, u32[]{:S(2)}) copy-start(bf16[1,2048,512]{2,1,0:T(8,128)(2,1)} %param.15) | copy-start | bytes 6291460
  77.7 40.2 %all-to-all-start.1 = ((bf16[16,32,1536]{2,1,0:T(8,128)(2,1)}), bf16[16,32,1536]{2,1,0:T(8,128)(2,1)}, u32[]{:S(2)}, u32[]{:S(2)}) async-start(bf16[16,32,1536]{2,1,0:T(8,128)(2,1)} %bitcast.49), calls=%async_computation.2 | async-start | bytes 3145728 | tf_op jit(solution)/shard_map/all_to_all | solution.py:37
  82.2 47.1 %reduce-scatter.2.cloned.1.call-start = ((), (), s32[]{:S(2)}) async-start(), calls=%async_computation.5 | async-start | bytes 3145728 | tf_op jit(solution)/shard_map/reduce_scatter | solution.py:44
  87.8 0.7 copy-start.4
  123.9 41.1 %all-to-all-start.2 = ((bf16[16,32,1536]{2,1,0:T(8,128)(2,1)}), bf16[16,32,1536]{2,1,0:T(8,128)(2,1)}, u32[]{:S(2)}, u32[]{:S(2)}) async-start(bf16[16,32,1536]{2,1,0:T(8,128)(2,1)} %broadcast_select_fusion), calls=%async_computation.3 | async-start | bytes 3145728 | tf_op jit(solution)/shard_map/all_to_all | solution.py:39
  164.9 30.3 %all-to-all-start = ((bf16[16,32,1024]{2,1,0:T(8,128)(2,1)}), bf16[16,32,1024]{2,1,0:T(8,128)(2,1)S(1)}, u32[]{:S(2)}, u32[]{:S(2)}) async-start(bf16[16,32,1024]{2,1,0:T(8,128)(2,1)} %bitcast.50), calls=%async_computation.1 | async-start | bytes 2097152 | tf_op jit(solution)/shard_map/all_to_all | solution.py:46
  170.4 5.1 %copy-start.2 = (bf16[2,512,2048]{2,1,0:T(8,128)(2,1)S(1)}, bf16[2,512,2048]{2,1,0:T(8,128)(2,1)}, u32[]{:S(2)}) copy-start(bf16[2,512,2048]{2,1,0:T(8,128)(2,1)} %all-gather.4.cloned.1.call-done) | copy-start | bytes 12582916
Sparse Core Ops, SparseCore 0:
  13.5 53.0 all-gather.3
  88.0 32.3 reduce-scatter.1
where the time goes:
time: 204 us; the launch traced here: 203 us
  waiting for transfers between devices  87.9 us (43%)
  blocking collectives  44.5 us (22%)
  matrix products  26.2 us (13%)
  starting transfers between devices  15.4 us (8%)
  between operations  14.1 us (7%)
  local copies, waits for them, and re-layouts  8.26 us (4%)
  other arithmetic  6.57 us (3%)
    all_to_all x1, waiting for transfers between devices, local(): lax.all_to_all(ordered, 'expert', split_axis=0, concat_axis=0, tiled=True)  35.6 us
    all_to_all x1, waiting for transfers between devices, local(): lax.all_to_all(packed, 'expert', split_axis=0, concat_axis=0, tiled=True)  29.4 us
    all_gather x1, blocking collectives, local(): routes_all = lax.all_gather(routes, 'expert', axis=0, tiled=True)  20.8 us
    all_gather x1, blocking collectives, local(): probs_all = lax.all_gather(probs, 'expert', axis=0, tiled=True)  18.5 us
    all_gather x1, waiting for transfers between devices, local(): both = lax.all_gather(both, 'expert', axis=1, tiled=True)  11.9 us
    all_to_all x1, waiting for transfers between devices, local(): lax.all_to_all(summed, 'expert', split_axis=0, concat_axis=0, tiled=True)  10.9 us
    all_to_all x1, starting transfers between devices, local(): lax.all_to_all(ordered, 'expert', split_axis=0, concat_axis=0, tiled=True)  5.42 us
    all_to_all x1, starting transfers between devices, local(): lax.all_to_all(summed, 'expert', split_axis=0, concat_axis=0, tiled=True)  5.41 us
  transfers between devices with their start and end apart: 5, of which 4 were waited for; matrix products, arithmetic and copies ran while one was open for 14% of the time, Pallas kernels for 0%

commit v1 on v0

--- a/solution.py
+++ b/solution.py
@@ -5,6 +5,24 @@
 
 contract_rows = (((0,), (0,)), ((), ()))
 contract_cols = (((1,), (1,)), ((), ()))
+
+
+def replace_object(dimension_no, load):
+    chips = lax.axis_size("expert")
+    made = []
+    for i in range(1, chips):
+        made.append((i - 1, i))
+    newest = made + [(chips - 1, 0)]
+    f_next = load
+    in_order = [f_next]
+    for _ in range(chips - 1):
+        f_next = lax.ppermute(f_next, "expert", newest)
+        in_order += [f_next]
+    return jnp.roll(
+        jnp.concatenate([*reversed(in_order)], dimension_no),
+        shift=(lax.axis_index("expert") + 1) * f_next.shape[dimension_no],
+        axis=dimension_no,
+    )
 
 
 def pair_rows(cotangent, routes, probs, expert):
@@ -19,7 +37,7 @@
     me = lax.axis_index("expert")
     w_gate, w_up, w_down = (gate_weight[0], up_weight[0], down_weight[0])
     routes_all = lax.all_gather(routes, "expert", axis=0, tiled=True)
-    probs_all = lax.all_gather(probs, "expert", axis=0, tiled=True)
+    probs_all = replace_object(0, probs)
     both = jnp.stack([tokens, cotangent], axis=0)
     both = lax.all_gather(both, "dp", axis=2, tiled=True)
     both = lax.all_gather(both, "expert", axis=1, tiled=True)

time: 204 us -> 253 us (1.24)
  waiting for transfers between devices: 87.9 us -> 119 us
  starting transfers between devices: 15.4 us -> 36.7 us
    ppermute x0 -> x15, waiting for transfers between devices: none -> 41.3 us  [replace_object(): f_next = lax.ppermute(f_next, 'expert', newest)]
    all_gather x1 -> x0, blocking collectives: 18.5 us -> none  [local(): probs_all = lax.all_gather(probs, 'expert', axis=0, tiled=True)]
    all_gather x1, blocking collectives: 20.8 us -> 37 us  [local(): routes_all = lax.all_gather(routes, 'expert', axis=0, tiled=True)]
    ppermute x0 -> x15, starting transfers between devices: none -> 13.2 us  [replace_object(): f_next = lax.ppermute(f_next, 'expert', newest)]
    all_gather x1, waiting for transfers between devices: 11.9 us -> 0.02 us  [local(): both = lax.all_gather(both, 'expert', axis=1, tiled=True)]
    all_to_all x1, starting transfers between devices: 4.52 us -> 12.7 us  [local(): lax.all_to_all(packed, 'expert', split_axis=0, concat_axis=0, tiled=True)]
  transfers between devices with their start and end apart: 5 -> 20, of which waited for: 4 -> 17; matrix products, arithmetic and copies ran while one was open for 14% -> 11% of each run, Pallas kernels for 0% -> 0%
where the time goes in v1:
time: 253 us; the launch traced here: 252 us
  waiting for transfers between devices  119 us (47%)
  blocking collectives  42.1 us (17%)
  starting transfers between devices  36.7 us (15%)
  matrix products  24 us (9%)
  between operations  14.2 us (6%)
  local copies, waits for them, and re-layouts  9.69 us (4%)
  other arithmetic  6.64 us (3%)
    ppermute x15, waiting for transfers between devices, replace_object(): f_next = lax.ppermute(f_next, 'expert', newest)  41.3 us
    all_gather x1, blocking collectives, local(): routes_all = lax.all_gather(routes, 'expert', axis=0, tiled=True)  37 us
    all_to_all x1, waiting for transfers between devices, local(): lax.all_to_all(ordered, 'expert', split_axis=0, concat_axis=0, tiled=True)  35.6 us
    all_to_all x1, waiting for transfers between devices, local(): lax.all_to_all(packed, 'expert', split_axis=0, concat_axis=0, tiled=True)  30.7 us
    ppermute x15, starting transfers between devices, replace_object(): f_next = lax.ppermute(f_next, 'expert', newest)  13.2 us
    all_to_all x1, starting transfers between devices, local(): lax.all_to_all(packed, 'expert', split_axis=0, concat_axis=0, tiled=True)  12.7 us
    all_to_all x1, waiting for transfers between devices, local(): lax.all_to_all(summed, 'expert', split_axis=0, concat_axis=0, tiled=True)  11 us
    all_to_all x1, starting transfers between devices, local(): lax.all_to_all(summed, 'expert', split_axis=0, concat_axis=0, tiled=True)  5.41 us
  transfers between devices with their start and end apart: 20, of which 17 were waited for; matrix products, arithmetic and copies ran while one was open for 11% of the time, Pallas kernels for 0%

profile of v1, /device:TPU:9, one launch (start us, length us, event | category | flops | bytes accessed | tf_op | source)
XLA Modules:
  0.0 252.0 jit_solution(179990245700705415)
XLA Ops:
  7.2 1.0 pad_maximum_fusion.1
  8.3 5.1 %all_gather.9 = bf16[2,32,2048]{2,1,0:T(8,128)(2,1)} all-gather(bf16[2,32,1024]{2,1,0:T(8,128)(2,1)S(1)} %pad_maximum_fusion.1), channel_id=1, replica_groups=mesh['dp'=2,'expert'=16] {'dp'}, dimensions={2}, use_global_device_ids=true | all-gather | bytes 393216 | tf_op jit(solution)/shard_map/all_gather | solution.py:42
  13.4 2.7 %collective-permute-start = (f32[32,8]{0,1:T(8,128)}, f32[32,8]{0,1:T(8,128)S(1)}, u32[]{:S(2)}, u32[]{:S(2)}) collective-permute-start(f32[32,8]{0,1:T(8,128)} %param.11), channel_id=1, source_target_pairs={{0,1},{1,2},{2,3},{3,4},{4,5},{5,6},{6,7},{7,8},{8,9},{9,10},{10,1... | collective-permute-start | bytes 3080 | tf_op jit(solution)/shard_map/ppermute | solution.py:19
  16.1 1.0 collective-permute-done
  17.1 2.3 collective-permute-start.1
  19.4 0.8 collective-permute-done.1
  20.1 2.3 collective-permute-start.2
  22.4 1.3 collective-permute-done.2
  23.7 1.7 collective-permute-start.3
  25.4 2.3 collective-permute-done.3
  27.8 0.7 collective-permute-start.4
  28.5 3.2 %collective-permute-done.4 = f32[32,8]{0,1:T(8,128)S(1)} collective-permute-done((f32[32,8]{0,1:T(8,128)S(1)}, f32[32,8]{0,1:T(8,128)S(1)}, u32[]{:S(2)}, u32[]{:S(2)}) %collective-permute-start.4) | collective-permute-done | bytes 1056 | tf_op jit(solution)/shard_map/ppermute | solution.py:19
  31.8 3.9 %collective-permute-done.5 = f32[32,8]{0,1:T(8,128)S(1)} collective-permute-done((f32[32,8]{0,1:T(8,128)S(1)}, f32[32,8]{0,1:T(8,128)S(1)}, u32[]{:S(2)}, u32[]{:S(2)}) %collective-permute-start.5) | collective-permute-done | bytes 1056 | tf_op jit(solution)/shard_map/ppermute | solution.py:19
  35.7 3.9 %collective-permute-done.6 = f32[32,8]{0,1:T(8,128)S(1)} collective-permute-done((f32[32,8]{0,1:T(8,128)S(1)}, f32[32,8]{0,1:T(8,128)S(1)}, u32[]{:S(2)}, u32[]{:S(2)}) %collective-permute-start.6) | collective-permute-done | bytes 1056 | tf_op jit(solution)/shard_map/ppermute | solution.py:19
  39.6 3.9 %collective-permute-done.7 = f32[32,8]{0,1:T(8,128)S(1)} collective-permute-done((f32[32,8]{0,1:T(8,128)S(1)}, f32[32,8]{0,1:T(8,128)S(1)}, u32[]{:S(2)}, u32[]{:S(2)}) %collective-permute-start.7) | collective-permute-done | bytes 1056 | tf_op jit(solution)/shard_map/ppermute | solution.py:19
  43.6 4.1 %collective-permute-done.8 = f32[32,8]{0,1:T(8,128)S(1)} collective-permute-done((f32[32,8]{0,1:T(8,128)S(1)}, f32[32,8]{0,1:T(8,128)S(1)}, u32[]{:S(2)}, u32[]{:S(2)}) %collective-permute-start.8) | collective-permute-done | bytes 1056 | tf_op jit(solution)/shard_map/ppermute | solution.py:19
  47.6 4.1 %collective-permute-done.9 = f32[32,8]{0,1:T(8,128)S(1)} collective-permute-done((f32[32,8]{0,1:T(8,128)S(1)}, f32[32,8]{0,1:T(8,128)S(1)}, u32[]{:S(2)}, u32[]{:S(2)}) %collective-permute-start.9) | collective-permute-done | bytes 1056 | tf_op jit(solution)/shard_map/ppermute | solution.py:19
  51.8 5.0 %collective-permute-done.10 = f32[32,8]{0,1:T(8,128)S(1)} collective-permute-done((f32[32,8]{0,1:T(8,128)S(1)}, f32[32,8]{0,1:T(8,128)S(1)}, u32[]{:S(2)}, u32[]{:S(2)}) %collective-permute-start.10) | collective-permute-done | bytes 1056 | tf_op jit(solution)/shard_map/ppermute | solution.py:19
  56.8 5.8 %collective-permute-done.11 = f32[32,8]{0,1:T(8,128)S(1)} collective-permute-done((f32[32,8]{0,1:T(8,128)S(1)}, f32[32,8]{0,1:T(8,128)S(1)}, u32[]{:S(2)}, u32[]{:S(2)}) %collective-permute-start.11) | collective-permute-done | bytes 1056 | tf_op jit(solution)/shard_map/ppermute | solution.py:19
  62.7 37.0 %all-gather = s32[16,32,8]{1,2,0:T(8,128)S(1)} all-gather(s32[1,32,8]{1,2,0:T(8,128)} %bitcast.56), channel_id=1, replica_groups=mesh['dp'=2,'expert'=16] {'expert'}, dimensions={0}, use_global_device_ids=true | all-gather | bytes 17408 | tf_op jit(solution)/shard_map/all_gather | solution.py:39
  99.6 1.2 dynamic_slice.8
  100.9 1.1 collective-permute-start.13
  102.0 0.7 broadcast_compare_fusion.1
  102.8 2.3 collective-permute-start.14
  105.3 1.7 collective-permute-done.14
  107.0 0.8 concatenate.9
  108.0 3.0 %fusion.9 = f32[512,512]{0,1:T(8,128)S(1)} fusion(bf16[1,2048,512]{2,1,0:T(8,128)(2,1)S(1)} %copy-done, bf16[2,512,2048]{2,1,0:T(8,128)(2,1)} %all-gather.3.cloned.1.call-done), kind=kOutput, calls=%fused_computation.15 | convolution fusion | flops 1073741824 | bytes 5242880 | tf_op jit(solution)/shard_map/dot_general | solution.py:46
  111.1 0.4 copy-done.3
  111.5 1.3 fusion.12
  112.8 0.3 copy-done.5
  113.1 1.7 multiply_convert_fusion
  114.8 1.2 pad_maximum_fusion
  116.1 2.6 %copy.19 = bf16[512,1536]{1,0:T(8,128)(2,1)} copy(bf16[512,1536]{0,1:T(8,128)(2,1)} %pad_maximum_fusion) | data formatting | bytes 3145728 | tf_op jit(solution)/shard_map/concatenate | solution.py:53
  118.6 12.7 %all-to-all-start.1 = ((bf16[16,32,1536]{2,1,0:T(8,128)(2,1)}), bf16[16,32,1536]{2,1,0:T(8,128)(2,1)}, u32[]{:S(2)}, u32[]{:S(2)}) async-start(bf16[16,32,1536]{2,1,0:T(8,128)(2,1)} %bitcast.52), calls=%async_computation.2 | async-start | bytes 3145728 | tf_op jit(solution)/shard_map/all_to_all | solution.py:55
  131.4 1.3 fusion.7
  133.0 2.6 %add_convert_fusion = bf16[512,2048]{1,0:T(8,128)(2,1)} fusion(f32[512,2048]{1,0:T(8,128)S(1)} %fusion.7, bf16[512,512]{0,1:T(8,128)(2,1)S(1)} %get-tuple-element.8, bf16[1,2048,512]{2,1,0:T(8,128)(2,1)S(1)} %copy-done.2), kind=kOutput, calls=%fused_computation.6 | convolution fusion | flops 1075838976 | bytes 8912896 | tf_op jit(solution)/shard_map/dot_general | solution.py:60
  135.6 0.6 copy-done.6
  136.3 30.7 %all-to-all-done.1 = bf16[16,32,1536]{2,1,0:T(8,128)(2,1)} async-done(((bf16[16,32,1536]{2,1,0:T(8,128)(2,1)}), bf16[16,32,1536]{2,1,0:T(8,128)(2,1)}, u32[]{:S(2)}, u32[]{:S(2)}) %all-to-all-start.1) | async-done | bytes 1572896 | tf_op jit(solution)/shard_map/all_to_all | solution.py:55
  167.0 3.2 %gather_fusion = bf16[16,32,1536]{2,1,0:T(8,128)(2,1)} fusion(bf16[16,32,1536]{2,1,0:T(8,128)(2,1)} %all-to-all-done.1, s32[1024]{0:T(1024)S(1)} %pad_clamp_fusion), kind=kCustom, calls=%fused_computation | custom fusion | bytes 3145792 | tf_op jit(solution)/shard_map/jit(_take)/gather | solution.py:56
  170.2 2.8 %broadcast_select_fusion = bf16[16,32,1536]{2,1,0:T(8,128)(2,1)} fusion(bf16[16,32,1536]{2,1,0:T(8,128)(2,1)} %gather_fusion, pred[16]{0:T(512)(128)(4,1)S(1)} %compare_and_fusion), kind=kLoop, calls=%fused_computation.26 | loop fusion | flops 786432 | bytes 3145744 | tf_op jit(solution)/shard_map/jit(_take)/select_n | solution.py:56
  173.0 5.4 %all-to-all-start.2 = ((bf16[16,32,1536]{2,1,0:T(8,128)(2,1)}), bf16[16,32,1536]{2,1,0:T(8,128)(2,1)}, u32[]{:S(2)}, u32[]{:S(2)}) async-start(bf16[16,32,1536]{2,1,0:T(8,128)(2,1)} %broadcast_select_fusion), calls=%async_computation.3 | async-start | bytes 3145728 | tf_op jit(solution)/shard_map/all_to_all | solution.py:57
  178.4 35.6 %all-to-all-done.2 = bf16[16,32,1536]{2,1,0:T(8,128)(2,1)} async-done(((bf16[16,32,1536]{2,1,0:T(8,128)(2,1)}), bf16[16,32,1536]{2,1,0:T(8,128)(2,1)}, u32[]{:S(2)}, u32[]{:S(2)}) %all-to-all-start.2) | async-done | bytes 1572896 | tf_op jit(solution)/shard_map/all_to_all | solution.py:57
  214.0 5.4 %all-to-all-start = ((bf16[16,32,1024]{2,1,0:T(8,128)(2,1)}), bf16[16,32,1024]{2,1,0:T(8,128)(2,1)S(1)}, u32[]{:S(2)}, u32[]{:S(2)}) async-start(bf16[16,32,1024]{2,1,0:T(8,128)(2,1)} %bitcast.53), calls=%async_computation.1 | async-start | bytes 2097152 | tf_op jit(solution)/shard_map/all_to_all | solution.py:64
  219.4 5.1 %convolution_bitcast_fusion.1 = f32[1,2048,512]{2,1,0:T(8,128)} fusion(bf16[2,512,2048]{2,1,0:T(8,128)(2,1)} %all-gather.3.cloned.1.call-done, bf16[512,1536]{1,0:T(8,128)(2,1)} %bitcast.10), kind=kOutput, calls=%fused_computation.8 | convolution fusion | flops 1073741824 | bytes 6815744 | tf_op jit(solution)/shard_map/dot_general | solution.py:71
  224.6 4.4 %convolution_bitcast_fusion.2 = f32[1,2048,512]{2,1,0:T(8,128)} fusion(bf16[2,512,2048]{2,1,0:T(8,128)(2,1)S(1)} %copy-done.4, bf16[512,1536]{1,0:T(8,128)(2,1)} %bitcast.10), kind=kOutput, calls=%fused_computation.9 | convolution fusion | flops 1073741824 | bytes 6815744 | tf_op jit(solution)/shard_map/dot_general | solution.py:68
  228.9 4.5 %convolution_bitcast_fusion = f32[1,2048,512]{2,1,0:T(8,128)} fusion(f32[512]{0:T(512)S(1)} %get-tuple-element.4, bf16[2,512,2048]{2,1,0:T(8,128)(2,1)S(1)} %copy-done.4, bf16[512,1536]{1,0:T(8,128)(2,1)} %bitcast.10), kind=kOutput, calls=%fused_computation.7 | convolution fusion | flops 1076887552 | bytes 6817792 | tf_op jit(solution)/shard_map/dot_general | solution.py:77
  233.4 11.0 %all-to-all-done = bf16[16,32,1024]{2,1,0:T(8,128)(2,1)S(1)} async-done(((bf16[16,32,1024]{2,1,0:T(8,128)(2,1)}), bf16[16,32,1024]{2,1,0:T(8,128)(2,1)S(1)}, u32[]{:S(2)}, u32[]{:S(2)}) %all-to-all-start) | async-done | bytes 1048608 | tf_op jit(solution)/shard_map/all_to_all | solution.py:64
  244.4 0.8 reduce_sum.31
  (35 shorter events, 0.9 us)
Async XLA Ops:
  7.2 100.8 %copy-start = (bf16[1,2048,512]{2,1,0:T(8,128)(2,1)S(1)}, bf16[1,2048,512]{2,1,0:T(8,128)(2,1)}, u32[]{:S(2)}) copy-start(bf16[1,2048,512]{2,1,0:T(8,128)(2,1)} %param.13) | copy-start | bytes 6291460
  7.2 100.8 %all-gather.3.cloned.1.call-start = ((), (), s32[]{:S(2)}) async-start(), calls=%async_computation.4 | async-start | bytes 4456448 | tf_op jit(solution)/shard_map/all_gather | solution.py:43
  13.4 3.7 %collective-permute-start = (f32[32,8]{0,1:T(8,128)}, f32[32,8]{0,1:T(8,128)S(1)}, u32[]{:S(2)}, u32[]{:S(2)}) collective-permute-start(f32[32,8]{0,1:T(8,128)} %param.11), channel_id=1, source_target_pairs={{0,1},{1,2},{2,3},{3,4},{4,5},{5,6},{6,7},{7,8},{8,9},{9,10},{10,1... | collective-permute-start | bytes 3080 | tf_op jit(solution)/shard_map/ppermute | solution.py:19
  17.1 3.0 %collective-permute-start.1 = (f32[32,8]{0,1:T(8,128)S(1)}, f32[32,8]{0,1:T(8,128)S(1)}, u32[]{:S(2)}, u32[]{:S(2)}) collective-permute-start(f32[32,8]{0,1:T(8,128)S(1)} %collective-permute-done), channel_id=1, source_target_pairs={{0,1},{1,2},{2,3},{3,4},{4,5},{5,6},{6,7},{7,8},{8,9},{9,10},{10,1... | collective-permute-start | bytes 3080 | tf_op jit(solution)/shard_map/ppermute | solution.py:19
  20.1 3.6 %collective-permute-start.2 = (f32[32,8]{0,1:T(8,128)S(1)}, f32[32,8]{0,1:T(8,128)S(1)}, u32[]{:S(2)}, u32[]{:S(2)}) collective-permute-start(f32[32,8]{0,1:T(8,128)S(1)} %collective-permute-done.1), channel_id=1, source_target_pairs={{0,1},{1,2},{2,3},{3,4},{4,5},{5,6},{6,7},{7,8},{8,9},{9,10},{10,1... | collective-permute-start | bytes 3080 | tf_op jit(solution)/shard_map/ppermute | solution.py:19
  23.7 4.0 %collective-permute-start.3 = (f32[32,8]{0,1:T(8,128)S(1)}, f32[32,8]{0,1:T(8,128)S(1)}, u32[]{:S(2)}, u32[]{:S(2)}) collective-permute-start(f32[32,8]{0,1:T(8,128)S(1)} %collective-permute-done.2), channel_id=1, source_target_pairs={{0,1},{1,2},{2,3},{3,4},{4,5},{5,6},{6,7},{7,8},{8,9},{9,10},{10,1... | collective-permute-start | bytes 3080 | tf_op jit(solution)/shard_map/ppermute | solution.py:19
  27.8 4.0 %collective-permute-start.4 = (f32[32,8]{0,1:T(8,128)S(1)}, f32[32,8]{0,1:T(8,128)S(1)}, u32[]{:S(2)}, u32[]{:S(2)}) collective-permute-start(f32[32,8]{0,1:T(8,128)S(1)} %collective-permute-done.3), channel_id=1, source_target_pairs={{0,1},{1,2},{2,3},{3,4},{4,5},{5,6},{6,7},{7,8},{8,9},{9,10},{10,1... | collective-permute-start | bytes 3080 | tf_op jit(solution)/shard_map/ppermute | solution.py:19
  31.8 3.9 %collective-permute-start.5 = (f32[32,8]{0,1:T(8,128)S(1)}, f32[32,8]{0,1:T(8,128)S(1)}, u32[]{:S(2)}, u32[]{:S(2)}) collective-permute-start(f32[32,8]{0,1:T(8,128)S(1)} %collective-permute-done.4), channel_id=1, source_target_pairs={{0,1},{1,2},{2,3},{3,4},{4,5},{5,6},{6,7},{7,8},{8,9},{9,10},{10,1... | collective-permute-start | bytes 3080 | tf_op jit(solution)/shard_map/ppermute | solution.py:19
  35.7 3.9 %collective-permute-start.6 = (f32[32,8]{0,1:T(8,128)S(1)}, f32[32,8]{0,1:T(8,128)S(1)}, u32[]{:S(2)}, u32[]{:S(2)}) collective-permute-start(f32[32,8]{0,1:T(8,128)S(1)} %collective-permute-done.5), channel_id=1, source_target_pairs={{0,1},{1,2},{2,3},{3,4},{4,5},{5,6},{6,7},{7,8},{8,9},{9,10},{10,1... | collective-permute-start | bytes 3080 | tf_op jit(solution)/shard_map/ppermute | solution.py:19
  39.6 3.9 %collective-permute-start.7 = (f32[32,8]{0,1:T(8,128)S(1)}, f32[32,8]{0,1:T(8,128)S(1)}, u32[]{:S(2)}, u32[]{:S(2)}) collective-permute-start(f32[32,8]{0,1:T(8,128)S(1)} %collective-permute-done.6), channel_id=1, source_target_pairs={{0,1},{1,2},{2,3},{3,4},{4,5},{5,6},{6,7},{7,8},{8,9},{9,10},{10,1... | collective-permute-start | bytes 3080 | tf_op jit(solution)/shard_map/ppermute | solution.py:19
  43.6 4.1 %collective-permute-start.8 = (f32[32,8]{0,1:T(8,128)S(1)}, f32[32,8]{0,1:T(8,128)S(1)}, u32[]{:S(2)}, u32[]{:S(2)}) collective-permute-start(f32[32,8]{0,1:T(8,128)S(1)} %collective-permute-done.7), channel_id=1, source_target_pairs={{0,1},{1,2},{2,3},{3,4},{4,5},{5,6},{6,7},{7,8},{8,9},{9,10},{10,1... | collective-permute-start | bytes 3080 | tf_op jit(solution)/shard_map/ppermute | solution.py:19
  47.6 4.1 %collective-permute-start.9 = (f32[32,8]{0,1:T(8,128)S(1)}, f32[32,8]{0,1:T(8,128)S(1)}, u32[]{:S(2)}, u32[]{:S(2)}) collective-permute-start(f32[32,8]{0,1:T(8,128)S(1)} %collective-permute-done.8), channel_id=1, source_target_pairs={{0,1},{1,2},{2,3},{3,4},{4,5},{5,6},{6,7},{7,8},{8,9},{9,10},{10,1... | collective-permute-start | bytes 3080 | tf_op jit(solution)/shard_map/ppermute | solution.py:19
  51.8 5.0 %collective-permute-start.10 = (f32[32,8]{0,1:T(8,128)S(1)}, f32[32,8]{0,1:T(8,128)S(1)}, u32[]{:S(2)}, u32[]{:S(2)}) collective-permute-start(f32[32,8]{0,1:T(8,128)S(1)} %collective-permute-done.9), channel_id=1, source_target_pairs={{0,1},{1,2},{2,3},{3,4},{4,5},{5,6},{6,7},{7,8},{8,9},{9,10},{10,1... | collective-permute-start | bytes 3080 | tf_op jit(solution)/shard_map/ppermute | solution.py:19
  56.8 5.8 %collective-permute-start.11 = (f32[32,8]{0,1:T(8,128)S(1)}, f32[32,8]{0,1:T(8,128)S(1)}, u32[]{:S(2)}, u32[]{:S(2)}) collective-permute-start(f32[32,8]{0,1:T(8,128)S(1)} %collective-permute-done.10), channel_id=1, source_target_pairs={{0,1},{1,2},{2,3},{3,4},{4,5},{5,6},{6,7},{7,8},{8,9},{9,10},{10,1... | collective-permute-start | bytes 3080 | tf_op jit(solution)/shard_map/ppermute | solution.py:19
  62.7 38.2 %collective-permute-start.12 = (f32[32,8]{0,1:T(8,128)S(1)}, f32[32,8]{0,1:T(8,128)S(1)}, u32[]{:S(2)}, u32[]{:S(2)}) collective-permute-start(f32[32,8]{0,1:T(8,128)S(1)} %collective-permute-done.11), channel_id=1, source_target_pairs={{0,1},{1,2},{2,3},{3,4},{4,5},{5,6},{6,7},{7,8},{8,9},{9,10},{10,1... | collective-permute-start | bytes 3080 | tf_op jit(solution)/shard_map/ppermute | solution.py:19
  100.9 1.9 collective-permute-start.13
  102.8 4.2 %collective-permute-start.14 = (f32[32,8]{0,1:T(8,128)S(1)}, f32[32,8]{0,1:T(8,128)S(1)}, u32[]{:S(2)}, u32[]{:S(2)}) collective-permute-start(f32[32,8]{0,1:T(8,128)S(1)} %collective-permute-done.13), channel_id=1, source_target_pairs={{0,1},{1,2},{2,3},{3,4},{4,5},{5,6},{6,7},{7,8},{8,9},{9,10},{10,1... | collective-permute-start | bytes 3080 | tf_op jit(solution)/shard_map/ppermute | solution.py:19
  108.0 3.1 %copy-start.1 = (bf16[1,2048,512]{2,1,0:T(8,128)(2,1)S(1)}, bf16[1,2048,512]{2,1,0:T(8,128)(2,1)}, u32[]{:S(2)}) copy-start(bf16[1,2048,512]{2,1,0:T(8,128)(2,1)} %param.14) | copy-start | bytes 6291460
  108.0 3.4 %copy-start.3 = (bf16[2,512,2048]{2,1,0:T(8,128)(2,1)S(1)}, bf16[2,512,2048]{2,1,0:T(8,128)(2,1)}, u32[]{:S(2)}) copy-start(bf16[2,512,2048]{2,1,0:T(8,128)(2,1)} %all-gather.3.cloned.1.call-done) | copy-start | bytes 12582916
  111.5 1.6 copy-start.5
  118.6 48.4 %all-to-all-start.1 = ((bf16[16,32,1536]{2,1,0:T(8,128)(2,1)}), bf16[16,32,1536]{2,1,0:T(8,128)(2,1)}, u32[]{:S(2)}, u32[]{:S(2)}) async-start(bf16[16,32,1536]{2,1,0:T(8,128)(2,1)} %bitcast.52), calls=%async_computation.2 | async-start | bytes 3145728 | tf_op jit(solution)/shard_map/all_to_all | solution.py:55
  131.3 47.0 %reduce-scatter.2.cloned.1.call-start = ((), (), s32[]{:S(2)}) async-start(), calls=%async_computation.5 | async-start | bytes 3145728 | tf_op jit(solution)/shard_map/reduce_scatter | solution.py:62
  131.4 1.6 copy-start.2
  135.6 0.7 copy-start.6
  173.0 41.0 %all-to-all-start.2 = ((bf16[16,32,1536]{2,1,0:T(8,128)(2,1)}), bf16[16,32,1536]{2,1,0:T(8,128)(2,1)}, u32[]{:S(2)}, u32[]{:S(2)}) async-start(bf16[16,32,1536]{2,1,0:T(8,128)(2,1)} %broadcast_select_fusion), calls=%async_computation.3 | async-start | bytes 3145728 | tf_op jit(solution)/shard_map/all_to_all | solution.py:57
  214.0 30.3 %all-to-all-start = ((bf16[16,32,1024]{2,1,0:T(8,128)(2,1)}), bf16[16,32,1024]{2,1,0:T(8,128)(2,1)S(1)}, u32[]{:S(2)}, u32[]{:S(2)}) async-start(bf16[16,32,1024]{2,1,0:T(8,128)(2,1)} %bitcast.53), calls=%async_computation.1 | async-start | bytes 2097152 | tf_op jit(solution)/shard_map/all_to_all | solution.py:64
  219.4 5.1 %copy-start.4 = (bf16[2,512,2048]{2,1,0:T(8,128)(2,1)S(1)}, bf16[2,512,2048]{2,1,0:T(8,128)(2,1)}, u32[]{:S(2)}) copy-start(bf16[2,512,2048]{2,1,0:T(8,128)(2,1)} %all-gather.3.cloned.1.call-done) | copy-start | bytes 12582916
Sparse Core Ops, SparseCore 0:
  13.5 53.0 all-gather.2
  135.7 32.5 reduce-scatter.1
